TPU v7x, 32 devices: a whole 2x2x4 slice. The times are simulated.
32 devices in a mesh: blk: 4 (over y, x), grp: 8 (over z, core).
Axes of the slice: x: 2, y: 2, z: 4, core: 2. Of those that a mesh axis runs over, the one named last changes fastest.
Arguments:
- h_blocks: bfloat16 [1536, 16, 128, 128], P(('blk', 'grp')), may hold values from -0.0625 to 0.0625
- h_cols: int32 [1536, 16], P(('blk', 'grp')), may hold values from 0 to 1535, as said below
- t_prev: bfloat16 [196608, 128], P(('blk', 'grp')), may hold values from -6 to 6
- t_cur: bfloat16 [196608, 128], P(('blk', 'grp')), may hold values from -6 to 6
- cheb_coeffs: float32 [3], replicated, may hold values from 0.4 to 1
- owner_slot: int32 [128], replicated, may hold values from 0 to 127, each once
Outputs:
- t_next: bfloat16 [196608, 128], P(('blk', 'grp'))
- t_last: bfloat16 [196608, 128], P(('blk', 'grp'))
- owner_density: float32 [128, 196608], P(('blk', 'grp'))
Inputs may be any that keep to these rules, and one draw needn't show every extreme that they name: Block column h_cols[i, k] lies within 24 block rows of i, counted around the ends (periodically); distances of exactly 24 occur both ways; a name may repeat within a row. `owner_slot`: each row of the owner layout receives exactly one window column.
All inputs are finite; a program needn't handle non-finite values.
Results may differ from a plain program's by a relative error of at most 0.009.
Values may be sent and summed in bfloat16 or wider, within the bound.
A program may use at most 192 MiB of HBM per device.

v0:
```python
import functools

import jax
import jax.numpy as jnp
from jax import lax
from jax.experimental import pallas as pl
from jax.experimental.pallas import tpu as pltpu
from jax.sharding import PartitionSpec as P

AXES = ("blk", "grp")

MESH = pl.DeviceIdType.MESH


def row_product(cols, row, h_ref, ext, cut):
    slots, last = h_ref.shape[1], ext.shape[0] - 1
    at = [cols[row, k] if cut == 0 else jnp.clip(cols[row, k] - cut, 0, last) for k in range(slots)]
    rhs = jnp.concatenate([ext[a] for a in at], axis=0)
    lhs = jnp.concatenate([h_ref[row, k] for k in range(slots)], axis=1)
    return jnp.dot(lhs, rhs, preferred_element_type=jnp.float32)


def whole_kernel(
    shape, h_cols, coeffs, owner, h_hbm, prev_hbm, cur_hbm, next_out, last_out, arrived,
    h_ref, ext_a, ext_b, ext_c, near_a, near_c, prev_ref, last_ref, packed, stage, chooser, cols,
    load_sem, h_sem, send_sem, recv_sem, move_sem, spread_sem, gather_sem, out_sem,
):
    reach, pieces, per_dev, group = shape
    rows, _, bs, width = h_ref.shape[0], h_ref.shape[1], h_ref.shape[2], ext_a.shape[2]
    piece = reach // pieces
    blks, grps = lax.axis_size("blk"), lax.axis_size("grp")
    devices = blks * grps
    blk, grp = lax.axis_index("blk"), lax.axis_index("grp")
    me = blk * grps + grp

    def place(linear):
        return (linear // grps, linear % grps)

    half = pieces // 2
    inner = half * piece
    first_side = grp % 2

    def middle_first(c):
        side = (first_side + c // half) % 2
        edge = c // pieces
        return side, edge, side * reach + spot(side, edge, c % half)

    def edge_first(c):
        side = (first_side + c // pieces) % 2
        edge = 1 - (c // half) % 2
        return side, edge, side * reach + spot(side, edge, c % half)

    def spot(side, edge, j):
        return ((edge + side + 1) % 2) * inner + j * piece

    def h_load(c):
        base = middle_first(c)[2]
        where = pl.ds(base, piece)
        return pltpu.make_async_copy(h_hbm.at[where], h_ref.at[where], h_sem.at[c])

    def halo(term, source, offset, full, near, where):
        side, edge, base = where
        there = (1 - 2 * side) * rows + base + reach
        if near is None:
            dest = full.at[pl.ds(there, piece)]
        else:
            dest = near.at[pl.ds(there - inner, piece)]
        slot = (base - side * reach) // piece
        return pltpu.make_async_remote_copy(
            src_ref=source.at[pl.ds(offset + base, piece)],
            dst_ref=dest,
            send_sem=send_sem.at[term, side, slot],
            recv_sem=recv_sem.at[term, side, slot],
            device_id=place((me + devices - 1 + 2 * side) % devices),
            device_id_type=MESH,
        )

    prev_load = pltpu.make_async_copy(prev_hbm, prev_ref, load_sem.at[0])
    cur_load = pltpu.make_async_copy(cur_hbm, ext_a.at[pl.ds(reach, rows)], load_sem.at[1])
    near_load = pltpu.make_async_copy(cur_hbm, near_a.at[pl.ds(inner, rows)], load_sem.at[2])
    near_load.start()
    cur_load.start()
    prev_load.start()

    barrier = pltpu.get_barrier_semaphore()

    def greet(i, carry):
        pl.semaphore_signal(barrier, inc=1, device_id=place((me + i) % devices), device_id_type=MESH)
        return carry

    lax.fori_loop(1, devices, greet, 0)
    for c in range(2 * pieces):
        h_load(c).start()

    q = lax.broadcasted_iota(jnp.int32, chooser.shape, 0)
    slot = (q % devices) * per_dev + q // devices
    chooser[...] = jnp.where(slot == owner[...], 1.0, 0.0).astype(chooser.dtype)

    pl.semaphore_wait(barrier, devices - 1)
    start_order = [edge_first(c) for c in range(2 * pieces)]
    edges = [c for c in range(2 * pieces) if (c // half) % 2 == 0]
    outers = [c for c in range(2 * pieces) if (c // half) % 2 == 1]
    for c in edges + outers:
        halo(0, cur_hbm, 0, ext_a, near_a if c in edges else None, start_order[c]).start()
    total_rows = rows * devices

    def local_row(row, carry):
        for k in range(h_ref.shape[1]):
            at = h_cols[k, row] - me * rows + reach
            at = jnp.where(at < 0, at + total_rows, at)
            at = jnp.where(at >= total_rows, at - total_rows, at)
            cols[row, k] = jnp.clip(at, 0, rows + 2 * reach - 1)
        return carry

    lax.fori_loop(0, rows, local_row, 0)
    prev_load.wait()
    cur_load.wait()
    near_load.wait()

    def rows_of(where, ext, cut, old, old_at, stores):
        for r in range(piece):
            row = where[2] + r
            total = row_product(cols, row, h_ref, ext, cut)
            fresh = 2.0 * total - old[old_at + row].astype(jnp.float32)
            for new, new_at in stores:
                new[new_at + row] = fresh.astype(new.dtype)

    def loop(low, high, order, ext, cut, old, old_at, stores, ready, done):
        def one_piece(c, carry):
            where = order(c)
            ready(c)
            rows_of(where, ext, cut, old, old_at, stores)
            done(c, where)
            return carry

        lax.fori_loop(low, high, one_piece, 0)

    def split_term(term, source, offset, ext, near, old, old_at, stores, ready, done):
        for c in edges:
            halo(term, source, offset, ext, near, start_order[c]).wait()
        moves = [
            pltpu.make_async_copy(near.at[pl.ds(0, inner)], ext.at[pl.ds(inner, inner)], move_sem.at[0]),
            pltpu.make_async_copy(
                near.at[pl.ds(inner + rows, inner)], ext.at[pl.ds(reach + rows, inner)], move_sem.at[1]
            ),
        ]
        for m in moves:
            m.start()
        loop(0, pieces, middle_first, near, inner, old, old_at, stores, ready, done)
        for m in moves:
            m.wait()
        for c in outers:
            halo(term, source, offset, ext, None, start_order[c]).wait()
        loop(pieces, 2 * pieces, middle_first, ext, 0, old, old_at, stores, ready, done)

    def nothing(c):
        pass

    split_term(
        0, cur_hbm, 0, ext_a, near_a, prev_ref, 0, [(ext_b, reach)],
        lambda c: h_load(c).wait(),
        lambda c, where: halo(1, ext_b, reach, ext_b, None, where).start(),
    )
    for c in range(2 * pieces):
        halo(1, ext_b, reach, ext_b, None, start_order[c]).wait()
    both = [(ext_c, reach), (near_c, inner)]
    for part in range(4):
        to_near = near_c if part % 2 == 0 else None
        loop(
            part * half, (part + 1) * half, edge_first, ext_b, 0, ext_a, reach, both, nothing,
            lambda c, where: halo(2, ext_c, reach, ext_c, to_near, where).start(),
        )
    next_store = pltpu.make_async_copy(ext_c.at[pl.ds(reach, rows)], next_out, out_sem.at[0])
    next_store.start()

    def pack(first):
        for b in range(group):
            row = first + b
            dens = coeffs[0] * ext_b[reach + row].astype(jnp.float32)
            dens = dens + coeffs[1] * ext_c[reach + row].astype(jnp.float32)
            dens = dens + coeffs[2] * last_ref[row].astype(jnp.float32)
            turned = lax.dot_general(
                chooser[...], dens.astype(jnp.bfloat16), (((1,), (1,)), ((), ())),
                preferred_element_type=jnp.float32,
            )
            for s in range(per_dev):
                stage[pl.ds(b * per_dev + s, devices, stride=group * per_dev), :] = turned[
                    s * devices : (s + 1) * devices
                ]
        span = group * per_dev
        tiles = stage[...].reshape(devices, span, bs).astype(packed.dtype)
        packed[:, pl.ds(pl.multiple_of(first * per_dev, span), span), :] = tiles

    def spread(base, count):
        where = pl.ds(base * per_dev, count * per_dev)

        def one(i, carry):
            k = i // blks
            turn = (grps // 2 + (1 - 2 * (k % 2)) * ((k + 1) // 2) + grps) % grps
            to_blk = (blk + i + 1) % blks
            to_grp = (grp + turn) % grps
            pltpu.make_async_remote_copy(
                src_ref=packed.at[to_blk * grps + to_grp, where],
                dst_ref=arrived.at[me, where],
                send_sem=spread_sem,
                recv_sem=gather_sem,
                device_id=(to_blk, to_grp),
                device_id_type=MESH,
            ).start()
            return carry

        lax.fori_loop(0, devices - 1, one, 0)

    interleaved = piece % group == 0

    def last_done(c, where):
        if interleaved:
            base = where[2]

            def one_group(g, carry):
                pack(base + g * group)
                return carry

            lax.fori_loop(0, piece // group, one_group, 0)

            @pl.when(c % half == 0)
            def _():
                spread(base, piece)

            if half > 1:

                @pl.when(c % half == half - 1)
                def _():
                    spread(base - (half - 2) * piece, (half - 1) * piece)

    split_term(2, ext_c, reach, ext_c, near_c, ext_b, reach, [(last_ref, 0)], nothing, last_done)
    last_store = pltpu.make_async_copy(last_ref, last_out, out_sem.at[1])
    last_store.start()
    if not interleaved:
        for g in range(rows // group):
            pack(g * group)
        spread(0, rows)
    own = pltpu.make_async_copy(packed.at[me], arrived.at[me], out_sem.at[2])
    own.start()
    everything = pltpu.make_async_remote_copy(
        src_ref=packed.at[pl.ds(0, devices - 1)],
        dst_ref=arrived.at[pl.ds(0, devices - 1)],
        send_sem=spread_sem,
        recv_sem=gather_sem,
        device_id=place((me + 1) % devices),
        device_id_type=MESH,
    )
    everything.wait()
    own.wait()
    next_store.wait()
    last_store.wait()


def in_hbm(array):
    return pltpu.with_memory_space_constraint(array, pltpu.HBM)


def finish_kernel(steps, next_ref, last_ref, arrived, next_out, last_out, owned, sems):
    copies = [
        pltpu.make_async_copy(next_ref, next_out, sems.at[0]),
        pltpu.make_async_copy(last_ref, last_out, sems.at[1]),
    ]

    @pl.when(pl.program_id(0) == 0)
    def _():
        for c in copies:
            c.start()

    owned[...] = arrived[...].astype(owned.dtype)

    @pl.when(pl.program_id(0) == steps - 1)
    def _():
        for c in copies:
            c.wait()


def finish(made_next, made_last, arrived):
    devices, span, bs = arrived.shape
    steps = 4
    anyspec = pl.BlockSpec(memory_space=pl.ANY)
    block = pl.BlockSpec((devices // steps, span, bs), lambda i: (i, 0, 0))
    term = jax.ShapeDtypeStruct(made_next.shape, made_next.dtype)
    return pl.pallas_call(
        functools.partial(finish_kernel, steps),
        out_shape=(term, term, jax.ShapeDtypeStruct(arrived.shape, jnp.float32)),
        grid=(steps,),
        in_specs=[anyspec, anyspec, block],
        out_specs=(anyspec, anyspec, block),
        scratch_shapes=[pltpu.SemaphoreType.DMA((2,))],
        compiler_params=pltpu.CompilerParams(vmem_limit_bytes=16 * 1024 * 1024),
        name="finish",
    )(made_next, made_last, arrived)


def on_device(h_blocks, h_cols, t_prev, t_cur, cheb_coeffs, owner_slot):
    rows, slots, bs, _ = h_blocks.shape
    width = t_cur.shape[1]
    devices = lax.axis_size(AXES)
    reach = rows // 2
    per_dev = width // devices
    pieces = next(p for p in (6, 2) if reach % p == 0)
    group = max(1, 16 // per_dev)
    group = group if rows % group == 0 else rows
    anyspec = pl.BlockSpec(memory_space=pl.ANY)
    hbm = pl.BlockSpec(memory_space=pltpu.HBM)
    smem = pl.BlockSpec(memory_space=pltpu.SMEM)
    vmem = pl.BlockSpec(memory_space=pltpu.VMEM)
    dma = pltpu.SemaphoreType.DMA
    term = jax.ShapeDtypeStruct((rows, bs, width), t_cur.dtype)
    ext = pltpu.VMEM((rows + 2 * reach, bs, width), t_cur.dtype)
    near = pltpu.VMEM((rows + reach, bs, width), t_cur.dtype)
    own = pltpu.VMEM((rows, bs, width), t_cur.dtype)
    made_next, made_last, arrived = pl.pallas_call(
        functools.partial(whole_kernel, (reach, pieces, per_dev, group)),
        out_shape=(term, term, jax.ShapeDtypeStruct((devices, rows * per_dev, bs), jnp.bfloat16)),
        in_specs=[smem, smem, vmem, hbm, hbm, hbm],
        out_specs=(anyspec, anyspec, anyspec),
        scratch_shapes=[
            pltpu.VMEM(h_blocks.shape, h_blocks.dtype),
            ext,
            ext,
            ext,
            near,
            near,
            own,
            own,
            pltpu.VMEM((devices, rows * per_dev, bs), jnp.bfloat16),
            pltpu.VMEM((devices * group * per_dev, bs), jnp.float32),
            pltpu.VMEM((width, width), jnp.bfloat16),
            pltpu.SMEM((rows, slots), jnp.int32),
            dma((3,)),
            dma((2 * pieces,)),
            dma((3, 2, pieces)),
            dma((3, 2, pieces)),
            dma((2,)),
            dma,
            dma,
            dma((3,)),
        ],
        compiler_params=pltpu.CompilerParams(collective_id=0, has_side_effects=True, vmem_limit_bytes=46 * 1024 * 1024),
        name="whole",
    )(
        in_hbm(h_cols.T),
        in_hbm(cheb_coeffs),
        in_hbm(owner_slot[None, :]),
        h_blocks,
        in_hbm(t_prev.reshape(rows, bs, width)),
        in_hbm(t_cur.reshape(rows, bs, width)),
    )
    made_next, made_last, owned = finish(made_next, made_last, arrived)
    owned = owned.reshape(devices * rows, per_dev, bs)
    owned = owned.transpose(1, 0, 2).reshape(per_dev, devices * rows * bs)
    return (made_next.reshape(-1, width), made_last.reshape(-1, width), owned)


def solution(mesh):
    return jax.shard_map(
        on_device,
        mesh=mesh,
        in_specs=(
            P(("blk", "grp"), None, None, None),
            P(("blk", "grp"), None),
            P(("blk", "grp"), None),
            P(("blk", "grp"), None),
            P(),
            P(),
        ),
        out_specs=(P(("blk", "grp"), None), P(("blk", "grp"), None), P(("blk", "grp"), None)),
        check_vma=False,
    )
```

profile of v0, /device:TPU:9, one launch (start us, length us, event | category | flops | bytes accessed | tf_op | source)
XLA Modules:
  0.0 98.7 jit_solution(7280277737467217901)
XLA Ops:
  0.6 94.9 %whole.1 = (bf16[48,128,128]{2,1,0:T(8,128)(2,1)S(1)}, bf16[48,128,128]{2,1,0:T(8,128)(2,1)S(1)}, bf16[32,192,128]{2,1,0:T(8,128)(2,1)S(1)}) custom-call(s32[16,48]{1,0:T(8,128)} %bitcast.13, f32[3]{0:T(128)} %coeffs.1, s32[1,128]{1,0:T(1,128)} %bitcast.14, bf16[48,16,128,128]{3,2,1,0:T(8,128)(2,1)} %h_hbm.1, bf16[48,128,128]{2,1,0:T(8,128)(2,1)} %bitcast.11, ...), custom_call_target="tpu_custom_call" | custom-call | tf_op jit(solution)/shard_map/whole/pallas_call | solution.py:318
  95.6 3.2 %finish.1 = (bf16[48,128,128]{2,1,0:T(8,128)(2,1)}, bf16[48,128,128]{2,1,0:T(8,128)(2,1)}, f32[32,192,128]{2,1,0:T(8,128)}) custom-call(bf16[48,128,128]{2,1,0:T(8,128)(2,1)S(1)} %get-tuple-element.9.next_ref, bf16[48,128,128]{2,1,0:T(8,128)(2,1)S(1)} %get-tuple-element.10.last_ref, bf16[32,192,128]{2,1,0:T(8,128)(2,1)S(1)} %get-tuple-element.11.arrived), custom_call_target="tpu_custom_call" | custom-call | tf_op jit(solution)/shard_map/finish/pallas_call | solution.py:288
where the time goes:
time: 100 us; the launch traced here: 98.7 us
  Pallas kernels  98.1 us (98%)
    pallas_call x1, Pallas kernels, on_device(): pl.pallas_call(functools.partial(whole_kernel, (reach, pieces, per_dev, g...  94.9 us
    pallas_call x1, Pallas kernels, finish(): pl.pallas_call(functools.partial(finish_kernel, steps), out_shape=(term,...  3.15 us

commit v1 on v0

--- a/solution.py
+++ b/solution.py
@@ -12,6 +12,14 @@
 MESH = pl.DeviceIdType.MESH
 
 
+def hops_of(devices):
+    hops, known = [], 1
+    while known < devices // 2:
+        hops.append(known)
+        known *= 2
+    return hops
+
+
 def row_product(cols, row, h_ref, ext, cut):
     slots, last = h_ref.shape[1], ext.shape[0] - 1
     at = [cols[row, k] if cut == 0 else jnp.clip(cols[row, k] - cut, 0, last) for k in range(slots)]
@@ -23,7 +31,7 @@
 def whole_kernel(
     shape, h_cols, coeffs, owner, h_hbm, prev_hbm, cur_hbm, next_out, last_out, arrived,
     h_ref, ext_a, ext_b, ext_c, near_a, near_c, prev_ref, last_ref, packed, stage, chooser, cols,
-    load_sem, h_sem, send_sem, recv_sem, move_sem, spread_sem, gather_sem, out_sem,
+    load_sem, h_sem, send_sem, recv_sem, move_sem, spread_sem, gather_sem, out_sem, meet_sem,
 ):
     reach, pieces, per_dev, group = shape
     rows, _, bs, width = h_ref.shape[0], h_ref.shape[1], h_ref.shape[2], ext_a.shape[2]
@@ -78,30 +86,46 @@
     prev_load = pltpu.make_async_copy(prev_hbm, prev_ref, load_sem.at[0])
     cur_load = pltpu.make_async_copy(cur_hbm, ext_a.at[pl.ds(reach, rows)], load_sem.at[1])
     near_load = pltpu.make_async_copy(cur_hbm, near_a.at[pl.ds(inner, rows)], load_sem.at[2])
+    barrier = pltpu.get_barrier_semaphore()
+
+    def signal_pair(semaphore, hop):
+        for other in (me + hop, me + devices - hop):
+            pl.semaphore_signal(semaphore, inc=1, device_id=place(other % devices), device_id_type=MESH)
+
+    signal_pair(barrier, 1)
+    cur_load.start()
     near_load.start()
-    cur_load.start()
     prev_load.start()
-
-    barrier = pltpu.get_barrier_semaphore()
-
-    def greet(i, carry):
-        pl.semaphore_signal(barrier, inc=1, device_id=place((me + i) % devices), device_id_type=MESH)
-        return carry
-
-    lax.fori_loop(1, devices, greet, 0)
-    for c in range(2 * pieces):
+    pl.semaphore_wait(barrier, 2)
+    start_order = [edge_first(c) for c in range(2 * pieces)]
+    edges = [c for c in range(2 * pieces) if (c // half) % 2 == 0]
+    outers = [c for c in range(2 * pieces) if (c // half) % 2 == 1]
+    for c in edges:
+        halo(0, cur_hbm, 0, ext_a, near_a, start_order[c]).start()
+    cur_load.wait()
+    for c in outers:
+        halo(0, ext_a, reach, ext_a, None, start_order[c]).start()
+    for c in range(pieces):
         h_load(c).start()
+
+    hops = hops_of(devices)
+
+    ahead = list(range(len(hops) + 1))
+
+    def meet():
+        if ahead:
+            step = ahead.pop(0)
+            if step > 0:
+                pl.semaphore_wait(meet_sem.at[step - 1], 2)
+            if step < len(hops):
+                signal_pair(meet_sem.at[step], hops[step])
+
+    meet()
 
     q = lax.broadcasted_iota(jnp.int32, chooser.shape, 0)
     slot = (q % devices) * per_dev + q // devices
     chooser[...] = jnp.where(slot == owner[...], 1.0, 0.0).astype(chooser.dtype)
 
-    pl.semaphore_wait(barrier, devices - 1)
-    start_order = [edge_first(c) for c in range(2 * pieces)]
-    edges = [c for c in range(2 * pieces) if (c // half) % 2 == 0]
-    outers = [c for c in range(2 * pieces) if (c // half) % 2 == 1]
-    for c in edges + outers:
-        halo(0, cur_hbm, 0, ext_a, near_a if c in edges else None, start_order[c]).start()
     total_rows = rows * devices
 
     def local_row(row, carry):
@@ -113,8 +137,10 @@
         return carry
 
     lax.fori_loop(0, rows, local_row, 0)
+    for c in range(pieces, 2 * pieces):
+        h_load(c).start()
+    meet()
     prev_load.wait()
-    cur_load.wait()
     near_load.wait()
 
     def rows_of(where, ext, cut, old, old_at, stores):
@@ -138,6 +164,7 @@
     def split_term(term, source, offset, ext, near, old, old_at, stores, ready, done):
         for c in edges:
             halo(term, source, offset, ext, near, start_order[c]).wait()
+        meet()
         moves = [
             pltpu.make_async_copy(near.at[pl.ds(0, inner)], ext.at[pl.ds(inner, inner)], move_sem.at[0]),
             pltpu.make_async_copy(
@@ -151,25 +178,30 @@
             m.wait()
         for c in outers:
             halo(term, source, offset, ext, None, start_order[c]).wait()
+        meet()
         loop(pieces, 2 * pieces, middle_first, ext, 0, old, old_at, stores, ready, done)
 
     def nothing(c):
         pass
 
     split_term(
-        0, cur_hbm, 0, ext_a, near_a, prev_ref, 0, [(ext_b, reach)],
+        0, ext_a, reach, ext_a, near_a, prev_ref, 0, [(ext_b, reach)],
         lambda c: h_load(c).wait(),
         lambda c, where: halo(1, ext_b, reach, ext_b, None, where).start(),
     )
+    meet()
     for c in range(2 * pieces):
         halo(1, ext_b, reach, ext_b, None, start_order[c]).wait()
     both = [(ext_c, reach), (near_c, inner)]
     for part in range(4):
         to_near = near_c if part % 2 == 0 else None
+        meet()
         loop(
             part * half, (part + 1) * half, edge_first, ext_b, 0, ext_a, reach, both, nothing,
             lambda c, where: halo(2, ext_c, reach, ext_c, to_near, where).start(),
         )
+    while ahead:
+        meet()
     next_store = pltpu.make_async_copy(ext_c.at[pl.ds(reach, rows)], next_out, out_sem.at[0])
     next_store.start()
 
@@ -223,15 +255,13 @@
 
             lax.fori_loop(0, piece // group, one_group, 0)
 
-            @pl.when(c % half == 0)
+            @pl.when(c == pieces - 1)
             def _():
-                spread(base, piece)
-
-            if half > 1:
-
-                @pl.when(c % half == half - 1)
-                def _():
-                    spread(base - (half - 2) * piece, (half - 1) * piece)
+                spread(inner, reach)
+
+            @pl.when((c >= pieces) & (c % half == half - 1))
+            def _():
+                spread(base - (half - 1) * piece, half * piece)
 
     split_term(2, ext_c, reach, ext_c, near_c, ext_b, reach, [(last_ref, 0)], nothing, last_done)
     last_store = pltpu.make_async_copy(last_ref, last_out, out_sem.at[1])
@@ -260,38 +290,38 @@
     return pltpu.with_memory_space_constraint(array, pltpu.HBM)
 
 
-def finish_kernel(steps, next_ref, last_ref, arrived, next_out, last_out, owned, sems):
+def finish_kernel(steps, next_ref, last_ref, arrived, next_out, last_out, owned, wide, sems):
     copies = [
         pltpu.make_async_copy(next_ref, next_out, sems.at[0]),
         pltpu.make_async_copy(last_ref, last_out, sems.at[1]),
     ]
-
-    @pl.when(pl.program_id(0) == 0)
-    def _():
-        for c in copies:
-            c.start()
-
-    owned[...] = arrived[...].astype(owned.dtype)
-
-    @pl.when(pl.program_id(0) == steps - 1)
-    def _():
-        for c in copies:
-            c.wait()
+    for c in copies:
+        c.start()
+    step = arrived.shape[0] // steps
+    for i in range(steps):
+        where = pl.ds(i * step, step)
+        wide[where] = arrived[where].astype(wide.dtype)
+        c = pltpu.make_async_copy(wide.at[where], owned.at[where], sems.at[2 + i])
+        c.start()
+        copies.append(c)
+    for c in copies:
+        c.wait()
 
 
 def finish(made_next, made_last, arrived):
-    devices, span, bs = arrived.shape
     steps = 4
     anyspec = pl.BlockSpec(memory_space=pl.ANY)
-    block = pl.BlockSpec((devices // steps, span, bs), lambda i: (i, 0, 0))
+    vmem = pl.BlockSpec(memory_space=pltpu.VMEM)
     term = jax.ShapeDtypeStruct(made_next.shape, made_next.dtype)
     return pl.pallas_call(
         functools.partial(finish_kernel, steps),
         out_shape=(term, term, jax.ShapeDtypeStruct(arrived.shape, jnp.float32)),
-        grid=(steps,),
-        in_specs=[anyspec, anyspec, block],
-        out_specs=(anyspec, anyspec, block),
-        scratch_shapes=[pltpu.SemaphoreType.DMA((2,))],
+        in_specs=[anyspec, anyspec, vmem],
+        out_specs=(anyspec, anyspec, anyspec),
+        scratch_shapes=[
+            pltpu.VMEM(arrived.shape, jnp.float32),
+            pltpu.SemaphoreType.DMA((2 + steps,)),
+        ],
         compiler_params=pltpu.CompilerParams(vmem_limit_bytes=16 * 1024 * 1024),
         name="finish",
     )(made_next, made_last, arrived)
@@ -341,6 +371,7 @@
             dma,
             dma,
             dma((3,)),
+            pltpu.SemaphoreType.REGULAR((len(hops_of(devices)),)),
         ],
         compiler_params=pltpu.CompilerParams(collective_id=0, has_side_effects=True, vmem_limit_bytes=46 * 1024 * 1024),
         name="whole",

time: 100 us -> 98.2 us (0.982)
  Pallas kernels: 98.1 us -> 97 us
where the time goes in v1:
time: 98.2 us; the launch traced here: 97.6 us
  Pallas kernels  97 us (99%)
    pallas_call x1, Pallas kernels, on_device(): pl.pallas_call(functools.partial(whole_kernel, (reach, pieces, per_dev, g...  94.2 us
    pallas_call x1, Pallas kernels, finish(): pl.pallas_call(functools.partial(finish_kernel, steps), out_shape=(term,...  2.72 us

profile of v1, /device:TPU:9, one launch (start us, length us, event | category | flops | bytes accessed | tf_op | source)
XLA Modules:
  0.0 97.6 jit_solution(11452620525390857683)
XLA Ops:
  0.6 94.2 %whole.1 = (bf16[48,128,128]{2,1,0:T(8,128)(2,1)S(1)}, bf16[48,128,128]{2,1,0:T(8,128)(2,1)S(1)}, bf16[32,192,128]{2,1,0:T(8,128)(2,1)S(1)}) custom-call(s32[16,48]{1,0:T(8,128)} %bitcast.13, f32[3]{0:T(128)} %coeffs.1, s32[1,128]{1,0:T(1,128)} %bitcast.14, bf16[48,16,128,128]{3,2,1,0:T(8,128)(2,1)} %h_hbm.1, bf16[48,128,128]{2,1,0:T(8,128)(2,1)} %bitcast.11, ...), custom_call_target="tpu_custom_call" | custom-call | tf_op jit(solution)/shard_map/whole/pallas_call | solution.py:348
  94.9 2.7 %finish.1 = (bf16[48,128,128]{2,1,0:T(8,128)(2,1)}, bf16[48,128,128]{2,1,0:T(8,128)(2,1)}, f32[32,192,128]{2,1,0:T(8,128)}) custom-call(bf16[48,128,128]{2,1,0:T(8,128)(2,1)S(1)} %get-tuple-element.9.next_ref, bf16[48,128,128]{2,1,0:T(8,128)(2,1)S(1)} %get-tuple-element.10.last_ref, bf16[32,192,128]{2,1,0:T(8,128)(2,1)S(1)} %get-tuple-element.11.arrived), custom_call_target="tpu_custom_call" | custom-call | tf_op jit(solution)/shard_map/finish/pallas_call | solution.py:316

commit v2 on v1

--- a/solution.py
+++ b/solution.py
@@ -29,9 +29,9 @@
 
 
 def whole_kernel(
-    shape, h_cols, coeffs, owner, h_hbm, prev_hbm, cur_hbm, next_out, last_out, arrived,
-    h_ref, ext_a, ext_b, ext_c, near_a, near_c, prev_ref, last_ref, packed, stage, chooser, cols,
-    load_sem, h_sem, send_sem, recv_sem, move_sem, spread_sem, gather_sem, out_sem, meet_sem,
+    shape, h_cols_hbm, coeffs_hbm, owner_hbm, h_hbm, prev_hbm, cur_hbm, next_out, last_out, arrived,
+    h_cols, coeffs, owner, h_ref, ext_a, ext_b, ext_c, near_a, near_c, prev_ref, last_ref, packed, stage, chooser, cols,
+    load_sem, h_sem, send_sem, recv_sem, move_sem, spread_sem, gather_sem, out_sem, meet_sem, small_sem,
 ):
     reach, pieces, per_dev, group = shape
     rows, _, bs, width = h_ref.shape[0], h_ref.shape[1], h_ref.shape[2], ext_a.shape[2]
@@ -61,10 +61,10 @@
     def spot(side, edge, j):
         return ((edge + side + 1) % 2) * inner + j * piece
 
-    def h_load(c):
-        base = middle_first(c)[2]
-        where = pl.ds(base, piece)
-        return pltpu.make_async_copy(h_hbm.at[where], h_ref.at[where], h_sem.at[c])
+    def h_load(g):
+        side = (first_side + g % 2) % 2
+        where = pl.ds(side * reach + spot(side, g // 2, 0), inner)
+        return pltpu.make_async_copy(h_hbm.at[where], h_ref.at[where], h_sem.at[g])
 
     def halo(term, source, offset, full, near, where):
         side, edge, base = where
@@ -73,15 +73,30 @@
             dest = full.at[pl.ds(there, piece)]
         else:
             dest = near.at[pl.ds(there - inner, piece)]
-        slot = (base - side * reach) // piece
         return pltpu.make_async_remote_copy(
             src_ref=source.at[pl.ds(offset + base, piece)],
             dst_ref=dest,
-            send_sem=send_sem.at[term, side, slot],
-            recv_sem=recv_sem.at[term, side, slot],
+            send_sem=send_sem.at[term],
+            recv_sem=recv_sem.at[term, side, edge],
             device_id=place((me + devices - 1 + 2 * side) % devices),
             device_id_type=MESH,
         )
+
+    def settle(term, copied, side, edge):
+        return pltpu.make_async_remote_copy(
+            src_ref=copied,
+            dst_ref=copied,
+            send_sem=send_sem.at[term],
+            recv_sem=recv_sem.at[term, side, edge],
+            device_id=place((me + 1) % devices),
+            device_id_type=MESH,
+        )
+
+    def landed(term, edge):
+        for side in range(2):
+            settle(term, ext_a.at[pl.ds(0, inner)], side, edge).wait_recv()
+
+    jump = (grp == 0) | (grp == grps - 1)
 
     prev_load = pltpu.make_async_copy(prev_hbm, prev_ref, load_sem.at[0])
     cur_load = pltpu.make_async_copy(cur_hbm, ext_a.at[pl.ds(reach, rows)], load_sem.at[1])
@@ -92,22 +107,43 @@
         for other in (me + hop, me + devices - hop):
             pl.semaphore_signal(semaphore, inc=1, device_id=place(other % devices), device_id_type=MESH)
 
+    small_loads = [
+        pltpu.make_async_copy(h_cols_hbm, h_cols, small_sem.at[0]),
+        pltpu.make_async_copy(coeffs_hbm, coeffs, small_sem.at[1]),
+        pltpu.make_async_copy(owner_hbm, owner, small_sem.at[2]),
+    ]
+
+    def loads():
+        near_load.start()
+        cur_load.start()
+        prev_load.start()
+
     signal_pair(barrier, 1)
-    cur_load.start()
-    near_load.start()
-    prev_load.start()
+    for c in small_loads:
+        c.start()
+    pl.when(jump)(loads)
     pl.semaphore_wait(barrier, 2)
     start_order = [edge_first(c) for c in range(2 * pieces)]
     edges = [c for c in range(2 * pieces) if (c // half) % 2 == 0]
     outers = [c for c in range(2 * pieces) if (c // half) % 2 == 1]
     for c in edges:
         halo(0, cur_hbm, 0, ext_a, near_a, start_order[c]).start()
+    pl.when(jnp.logical_not(jump))(loads)
+
+    def send_outers():
+        for c in outers[:half]:
+            halo(0, cur_hbm, 0, ext_a, None, start_order[c]).start()
+
+    send_outers()
+    for c in outers[half:]:
+        halo(0, cur_hbm, 0, ext_a, None, start_order[c]).start()
     cur_load.wait()
-    for c in outers:
-        halo(0, ext_a, reach, ext_a, None, start_order[c]).start()
-    for c in range(pieces):
-        h_load(c).start()
-
+    near_load.wait()
+    prev_load.wait()
+    for g in range(2):
+        h_load(g).start()
+    for c in small_loads:
+        c.wait()
     hops = hops_of(devices)
 
     ahead = list(range(len(hops) + 1))
@@ -137,11 +173,9 @@
         return carry
 
     lax.fori_loop(0, rows, local_row, 0)
-    for c in range(pieces, 2 * pieces):
-        h_load(c).start()
+    for g in range(2, 4):
+        h_load(g).start()
     meet()
-    prev_load.wait()
-    near_load.wait()
 
     def rows_of(where, ext, cut, old, old_at, stores):
         for r in range(piece):
@@ -161,10 +195,8 @@
 
         lax.fori_loop(low, high, one_piece, 0)
 
-    def split_term(term, source, offset, ext, near, old, old_at, stores, ready, done):
-        for c in edges:
-            halo(term, source, offset, ext, near, start_order[c]).wait()
-        meet()
+    def split_term(term, ext, near, old, old_at, stores, ready, done):
+        landed(term, 1)
         moves = [
             pltpu.make_async_copy(near.at[pl.ds(0, inner)], ext.at[pl.ds(inner, inner)], move_sem.at[0]),
             pltpu.make_async_copy(
@@ -173,37 +205,45 @@
         ]
         for m in moves:
             m.start()
+        while term == 2 and ahead:
+            meet()
         loop(0, pieces, middle_first, near, inner, old, old_at, stores, ready, done)
         for m in moves:
             m.wait()
-        for c in outers:
-            halo(term, source, offset, ext, None, start_order[c]).wait()
-        meet()
+        landed(term, 0)
         loop(pieces, 2 * pieces, middle_first, ext, 0, old, old_at, stores, ready, done)
 
     def nothing(c):
         pass
 
+    def h_ready(c):
+        @pl.when(c % half == 0)
+        def _():
+            h_load(c // half).wait()
+
     split_term(
-        0, ext_a, reach, ext_a, near_a, prev_ref, 0, [(ext_b, reach)],
-        lambda c: h_load(c).wait(),
+        0, ext_a, near_a, prev_ref, 0, [(ext_b, reach)], h_ready,
         lambda c, where: halo(1, ext_b, reach, ext_b, None, where).start(),
     )
     meet()
-    for c in range(2 * pieces):
-        halo(1, ext_b, reach, ext_b, None, start_order[c]).wait()
+    landed(1, 1)
+    landed(1, 0)
     both = [(ext_c, reach), (near_c, inner)]
     for part in range(4):
         to_near = near_c if part % 2 == 0 else None
-        meet()
+        if part % 2 == 1:
+            meet()
         loop(
             part * half, (part + 1) * half, edge_first, ext_b, 0, ext_a, reach, both, nothing,
             lambda c, where: halo(2, ext_c, reach, ext_c, to_near, where).start(),
         )
-    while ahead:
-        meet()
     next_store = pltpu.make_async_copy(ext_c.at[pl.ds(reach, rows)], next_out, out_sem.at[0])
     next_store.start()
+
+    interleaved = piece % group == 0
+
+    def place_of(row):
+        return jnp.where(row < rows - inner, row + inner, row + inner - rows) if interleaved else row
 
     def pack(first):
         for b in range(group):
@@ -220,8 +260,9 @@
                     s * devices : (s + 1) * devices
                 ]
         span = group * per_dev
+        at = place_of(first)
         tiles = stage[...].reshape(devices, span, bs).astype(packed.dtype)
-        packed[:, pl.ds(pl.multiple_of(first * per_dev, span), span), :] = tiles
+        packed[:, pl.ds(pl.multiple_of(at * per_dev, span), span), :] = tiles
 
     def spread(base, count):
         where = pl.ds(base * per_dev, count * per_dev)
@@ -243,8 +284,6 @@
 
         lax.fori_loop(0, devices - 1, one, 0)
 
-    interleaved = piece % group == 0
-
     def last_done(c, where):
         if interleaved:
             base = where[2]
@@ -257,13 +296,13 @@
 
             @pl.when(c == pieces - 1)
             def _():
-                spread(inner, reach)
-
-            @pl.when((c >= pieces) & (c % half == half - 1))
+                spread(reach, reach)
+
+            @pl.when(c == 2 * pieces - 1)
             def _():
-                spread(base - (half - 1) * piece, half * piece)
-
-    split_term(2, ext_c, reach, ext_c, near_c, ext_b, reach, [(last_ref, 0)], nothing, last_done)
+                spread(0, reach)
+
+    split_term(2, ext_c, near_c, ext_b, reach, [(last_ref, 0)], nothing, last_done)
     last_store = pltpu.make_async_copy(last_ref, last_out, out_sem.at[1])
     last_store.start()
     if not interleaved:
@@ -281,6 +320,8 @@
         device_id_type=MESH,
     )
     everything.wait()
+    for term in range(3):
+        settle(term, ext_b.at[pl.ds(reach, rows)], 0, 0).wait_send()
     own.wait()
     next_store.wait()
     last_store.wait()
@@ -290,7 +331,7 @@
     return pltpu.with_memory_space_constraint(array, pltpu.HBM)
 
 
-def finish_kernel(steps, next_ref, last_ref, arrived, next_out, last_out, owned, wide, sems):
+def finish_kernel(steps, turn, next_ref, last_ref, arrived, next_out, last_out, owned, wide, sems):
     copies = [
         pltpu.make_async_copy(next_ref, next_out, sems.at[0]),
         pltpu.make_async_copy(last_ref, last_out, sems.at[1]),
@@ -300,7 +341,12 @@
     step = arrived.shape[0] // steps
     for i in range(steps):
         where = pl.ds(i * step, step)
-        wide[where] = arrived[where].astype(wide.dtype)
+        if turn:
+            span = arrived.shape[1]
+            wide[where, pl.ds(0, span - turn)] = arrived[where, pl.ds(turn, span - turn)].astype(wide.dtype)
+            wide[where, pl.ds(span - turn, turn)] = arrived[where, pl.ds(0, turn)].astype(wide.dtype)
+        else:
+            wide[where] = arrived[where].astype(wide.dtype)
         c = pltpu.make_async_copy(wide.at[where], owned.at[where], sems.at[2 + i])
         c.start()
         copies.append(c)
@@ -308,13 +354,13 @@
         c.wait()
 
 
-def finish(made_next, made_last, arrived):
+def finish(made_next, made_last, arrived, turn):
     steps = 4
     anyspec = pl.BlockSpec(memory_space=pl.ANY)
     vmem = pl.BlockSpec(memory_space=pltpu.VMEM)
     term = jax.ShapeDtypeStruct(made_next.shape, made_next.dtype)
     return pl.pallas_call(
-        functools.partial(finish_kernel, steps),
+        functools.partial(finish_kernel, steps, turn),
         out_shape=(term, term, jax.ShapeDtypeStruct(arrived.shape, jnp.float32)),
         in_specs=[anyspec, anyspec, vmem],
         out_specs=(anyspec, anyspec, anyspec),
@@ -336,10 +382,10 @@
     pieces = next(p for p in (6, 2) if reach % p == 0)
     group = max(1, 16 // per_dev)
     group = group if rows % group == 0 else rows
+    piece = reach // pieces
+    turn = pieces // 2 * piece * per_dev if piece % group == 0 else 0
     anyspec = pl.BlockSpec(memory_space=pl.ANY)
     hbm = pl.BlockSpec(memory_space=pltpu.HBM)
-    smem = pl.BlockSpec(memory_space=pltpu.SMEM)
-    vmem = pl.BlockSpec(memory_space=pltpu.VMEM)
     dma = pltpu.SemaphoreType.DMA
     term = jax.ShapeDtypeStruct((rows, bs, width), t_cur.dtype)
     ext = pltpu.VMEM((rows + 2 * reach, bs, width), t_cur.dtype)
@@ -348,9 +394,12 @@
     made_next, made_last, arrived = pl.pallas_call(
         functools.partial(whole_kernel, (reach, pieces, per_dev, group)),
         out_shape=(term, term, jax.ShapeDtypeStruct((devices, rows * per_dev, bs), jnp.bfloat16)),
-        in_specs=[smem, smem, vmem, hbm, hbm, hbm],
+        in_specs=[hbm] * 6,
         out_specs=(anyspec, anyspec, anyspec),
         scratch_shapes=[
+            pltpu.SMEM((slots, rows), jnp.int32),
+            pltpu.SMEM(cheb_coeffs.shape, cheb_coeffs.dtype),
+            pltpu.VMEM((1, width), jnp.int32),
             pltpu.VMEM(h_blocks.shape, h_blocks.dtype),
             ext,
             ext,
@@ -364,14 +413,15 @@
             pltpu.VMEM((width, width), jnp.bfloat16),
             pltpu.SMEM((rows, slots), jnp.int32),
             dma((3,)),
-            dma((2 * pieces,)),
-            dma((3, 2, pieces)),
-            dma((3, 2, pieces)),
+            dma((4,)),
+            dma((3,)),
+            dma((3, 2, 2)),
             dma((2,)),
             dma,
             dma,
             dma((3,)),
             pltpu.SemaphoreType.REGULAR((len(hops_of(devices)),)),
+            dma((3,)),
         ],
         compiler_params=pltpu.CompilerParams(collective_id=0, has_side_effects=True, vmem_limit_bytes=46 * 1024 * 1024),
         name="whole",
@@ -383,7 +433,7 @@
         in_hbm(t_prev.reshape(rows, bs, width)),
         in_hbm(t_cur.reshape(rows, bs, width)),
     )
-    made_next, made_last, owned = finish(made_next, made_last, arrived)
+    made_next, made_last, owned = finish(made_next, made_last, arrived, turn)
     owned = owned.reshape(devices * rows, per_dev, bs)
     owned = owned.transpose(1, 0, 2).reshape(per_dev, devices * rows * bs)
     return (made_next.reshape(-1, width), made_last.reshape(-1, width), owned)

time: 98.2 us -> 95.8 us (0.976)
  Pallas kernels: 97 us -> 95 us
    pallas_call x1, Pallas kernels: 94.2 us -> 92.2 us  [on_device(): pl.pallas_call(functools.partial(whole_kernel, (reach, pieces, per_dev, g...]
where the time goes in v2:
time: 95.8 us; the launch traced here: 95.6 us
  Pallas kernels  95 us (99%)
    pallas_call x1, Pallas kernels, on_device(): pl.pallas_call(functools.partial(whole_kernel, (reach, pieces, per_dev, g...  92.2 us
    pallas_call x1, Pallas kernels, finish(): pl.pallas_call(functools.partial(finish_kernel, steps, turn), out_shape=(...  2.72 us

profile of v2, /device:TPU:9, one launch (start us, length us, event | category | flops | bytes accessed | tf_op | source)
XLA Modules:
  0.0 95.6 jit_solution(12895712562940202009)
XLA Ops:
  0.6 92.2 %whole.1 = (bf16[48,128,128]{2,1,0:T(8,128)(2,1)S(1)}, bf16[48,128,128]{2,1,0:T(8,128)(2,1)S(1)}, bf16[32,192,128]{2,1,0:T(8,128)(2,1)S(1)}) custom-call(s32[16,48]{1,0:T(8,128)} %bitcast.13, f32[3]{0:T(128)} %coeffs_hbm.1, s32[1,128]{1,0:T(1,128)} %bitcast.14, bf16[48,16,128,128]{3,2,1,0:T(8,128)(2,1)} %h_hbm.1, bf16[48,128,128]{2,1,0:T(8,128)(2,1)} %bitcast.11, ...), custom_call_target="tpu_custom_call" | custom-call | tf_op jit(solution)/shard_map/whole/pallas_call | solution.py:394
  92.9 2.7 %finish.1 = (bf16[48,128,128]{2,1,0:T(8,128)(2,1)}, bf16[48,128,128]{2,1,0:T(8,128)(2,1)}, f32[32,192,128]{2,1,0:T(8,128)}) custom-call(bf16[48,128,128]{2,1,0:T(8,128)(2,1)S(1)} %get-tuple-element.9.next_ref, bf16[48,128,128]{2,1,0:T(8,128)(2,1)S(1)} %get-tuple-element.10.last_ref, bf16[32,192,128]{2,1,0:T(8,128)(2,1)S(1)} %get-tuple-element.11.arrived), custom_call_target="tpu_custom_call" | custom-call | tf_op jit(solution)/shard_map/finish/pallas_call | solution.py:362

commit v3 on v2

--- a/solution.py
+++ b/solution.py
@@ -31,7 +31,7 @@
 def whole_kernel(
     shape, h_cols_hbm, coeffs_hbm, owner_hbm, h_hbm, prev_hbm, cur_hbm, next_out, last_out, arrived,
     h_cols, coeffs, owner, h_ref, ext_a, ext_b, ext_c, near_a, near_c, prev_ref, last_ref, packed, stage, chooser, cols,
-    load_sem, h_sem, send_sem, recv_sem, move_sem, spread_sem, gather_sem, out_sem, meet_sem, small_sem,
+    load_sem, h_sem, send_sem, recv_sem, move_sem, spread_sem, gather_sem, out_sem, meet_sem, small_sem, go_sem,
 ):
     reach, pieces, per_dev, group = shape
     rows, _, bs, width = h_ref.shape[0], h_ref.shape[1], h_ref.shape[2], ext_a.shape[2]
@@ -126,7 +126,12 @@
     start_order = [edge_first(c) for c in range(2 * pieces)]
     edges = [c for c in range(2 * pieces) if (c // half) % 2 == 0]
     outers = [c for c in range(2 * pieces) if (c // half) % 2 == 1]
-    for c in edges:
+    def send_edges():
+        for c in edges[:half]:
+            halo(0, cur_hbm, 0, ext_a, near_a, start_order[c]).start()
+
+    pl.when(jnp.logical_not(jump))(send_edges)
+    for c in edges[half:]:
         halo(0, cur_hbm, 0, ext_a, near_a, start_order[c]).start()
     pl.when(jnp.logical_not(jump))(loads)
 
@@ -134,7 +139,7 @@
         for c in outers[:half]:
             halo(0, cur_hbm, 0, ext_a, None, start_order[c]).start()
 
-    send_outers()
+    pl.when(jnp.logical_not(jump))(send_outers)
     for c in outers[half:]:
         halo(0, cur_hbm, 0, ext_a, None, start_order[c]).start()
     cur_load.wait()
@@ -177,6 +182,12 @@
         h_load(g).start()
     meet()
 
+    @pl.when(jump)
+    def _():
+        pl.semaphore_wait(go_sem, 1)
+        send_edges()
+        send_outers()
+
     def rows_of(where, ext, cut, old, old_at, stores):
         for r in range(piece):
             row = where[2] + r
@@ -205,12 +216,17 @@
         ]
         for m in moves:
             m.start()
-        while term == 2 and ahead:
-            meet()
         loop(0, pieces, middle_first, near, inner, old, old_at, stores, ready, done)
         for m in moves:
             m.wait()
+        if term == 0:
+            meet()
         landed(term, 0)
+        if term == 0:
+
+            @pl.when((grp == 1) | (grp == grps - 2))
+            def _():
+                pl.semaphore_signal(go_sem, inc=1, device_id=place(me + 1 - 2 * (grp % 2)), device_id_type=MESH)
         loop(pieces, 2 * pieces, middle_first, ext, 0, old, old_at, stores, ready, done)
 
     def nothing(c):
@@ -231,12 +247,12 @@
     both = [(ext_c, reach), (near_c, inner)]
     for part in range(4):
         to_near = near_c if part % 2 == 0 else None
-        if part % 2 == 1:
-            meet()
         loop(
             part * half, (part + 1) * half, edge_first, ext_b, 0, ext_a, reach, both, nothing,
             lambda c, where: halo(2, ext_c, reach, ext_c, to_near, where).start(),
         )
+    while ahead:
+        meet()
     next_store = pltpu.make_async_copy(ext_c.at[pl.ds(reach, rows)], next_out, out_sem.at[0])
     next_store.start()
 
@@ -269,9 +285,13 @@
 
         def one(i, carry):
             k = i // blks
-            turn = (grps // 2 + (1 - 2 * (k % 2)) * ((k + 1) // 2) + grps) % grps
+            far = grps // 2
+            low = (k + far - 1) % far
+            high = far + (k + 3) % far
+            first = jnp.where(grp < far, high, low)
+            near = jnp.where(grp < far, 0, far) + (grp + 1 + k) % far
             to_blk = (blk + i + 1) % blks
-            to_grp = (grp + turn) % grps
+            to_grp = jnp.where(k < far, first, near)
             pltpu.make_async_remote_copy(
                 src_ref=packed.at[to_blk * grps + to_grp, where],
                 dst_ref=arrived.at[me, where],
@@ -422,6 +442,7 @@
             dma((3,)),
             pltpu.SemaphoreType.REGULAR((len(hops_of(devices)),)),
             dma((3,)),
+            pltpu.SemaphoreType.REGULAR,
         ],
         compiler_params=pltpu.CompilerParams(collective_id=0, has_side_effects=True, vmem_limit_bytes=46 * 1024 * 1024),
         name="whole",

time: 95.8 us -> 93.7 us (0.978); the launches traced: 95.6 us -> 92.3 us
  Pallas kernels: 95 us -> 91.6 us
    pallas_call x1, Pallas kernels: 92.2 us -> 88.9 us  [on_device(): pl.pallas_call(functools.partial(whole_kernel, (reach, pieces, per_dev, g...]
where the time goes in v3:
time: 93.7 us; the launch traced here: 92.3 us
  Pallas kernels  91.6 us (98%)
    pallas_call x1, Pallas kernels, on_device(): pl.pallas_call(functools.partial(whole_kernel, (reach, pieces, per_dev, g...  88.9 us
    pallas_call x1, Pallas kernels, finish(): pl.pallas_call(functools.partial(finish_kernel, steps, turn), out_shape=(...  2.72 us

profile of v3, /device:TPU:9, one launch (start us, length us, event | category | flops | bytes accessed | tf_op | source)
XLA Modules:
  0.0 92.3 jit_solution(9928380971999225391)
XLA Ops:
  0.6 88.9 %whole.1 = (bf16[48,128,128]{2,1,0:T(8,128)(2,1)S(1)}, bf16[48,128,128]{2,1,0:T(8,128)(2,1)S(1)}, bf16[32,192,128]{2,1,0:T(8,128)(2,1)S(1)}) custom-call(s32[16,48]{1,0:T(8,128)} %bitcast.13, f32[3]{0:T(128)} %coeffs_hbm.1, s32[1,128]{1,0:T(1,128)} %bitcast.14, bf16[48,16,128,128]{3,2,1,0:T(8,128)(2,1)} %h_hbm.1, bf16[48,128,128]{2,1,0:T(8,128)(2,1)} %bitcast.11, ...), custom_call_target="tpu_custom_call" | custom-call | tf_op jit(solution)/shard_map/whole/pallas_call | solution.py:414
  89.6 2.7 %finish.1 = (bf16[48,128,128]{2,1,0:T(8,128)(2,1)}, bf16[48,128,128]{2,1,0:T(8,128)(2,1)}, f32[32,192,128]{2,1,0:T(8,128)}) custom-call(bf16[48,128,128]{2,1,0:T(8,128)(2,1)S(1)} %get-tuple-element.9.next_ref, bf16[48,128,128]{2,1,0:T(8,128)(2,1)S(1)} %get-tuple-element.10.last_ref, bf16[32,192,128]{2,1,0:T(8,128)(2,1)S(1)} %get-tuple-element.11.arrived), custom_call_target="tpu_custom_call" | custom-call | tf_op jit(solution)/shard_map/finish/pallas_call | solution.py:382

commit v4 on v3

--- a/solution.py
+++ b/solution.py
@@ -216,17 +216,18 @@
         ]
         for m in moves:
             m.start()
-        loop(0, pieces, middle_first, near, inner, old, old_at, stores, ready, done)
+        loop(0, half + 2, middle_first, near, inner, old, old_at, stores, ready, done)
+        if term == 0:
+
+            @pl.when((grp == 1) | (grp == grps - 2))
+            def _():
+                pl.semaphore_signal(go_sem, inc=1, device_id=place(me + 1 - 2 * (grp % 2)), device_id_type=MESH)
+        loop(half + 2, pieces, middle_first, near, inner, old, old_at, stores, ready, done)
         for m in moves:
             m.wait()
         if term == 0:
             meet()
         landed(term, 0)
-        if term == 0:
-
-            @pl.when((grp == 1) | (grp == grps - 2))
-            def _():
-                pl.semaphore_signal(go_sem, inc=1, device_id=place(me + 1 - 2 * (grp % 2)), device_id_type=MESH)
         loop(pieces, 2 * pieces, middle_first, ext, 0, old, old_at, stores, ready, done)
 
     def nothing(c):
@@ -287,7 +288,7 @@
             k = i // blks
             far = grps // 2
             low = (k + far - 1) % far
-            high = far + (k + 3) % far
+            high = far + (k + 1) % far
             first = jnp.where(grp < far, high, low)
             near = jnp.where(grp < far, 0, far) + (grp + 1 + k) % far
             to_blk = (blk + i + 1) % blks

time: 93.7 us -> 93.5 us (level)
  the two profiles are of different devices: /device:TPU:9 before, /device:TPU:8 now
where the time goes in v4:
time: 93.5 us; the launch traced here: 93.4 us
  Pallas kernels  92.7 us (99%)
    pallas_call x1, Pallas kernels, on_device(): pl.pallas_call(functools.partial(whole_kernel, (reach, pieces, per_dev, g...  90 us
    pallas_call x1, Pallas kernels, finish(): pl.pallas_call(functools.partial(finish_kernel, steps, turn), out_shape=(...  2.72 us

profile of v4, /device:TPU:8, one launch (start us, length us, event | category | flops | bytes accessed | tf_op | source)
XLA Modules:
  0.0 93.4 jit_solution(9145143566652309226)
XLA Ops:
  0.6 90.0 %whole.1 = (bf16[48,128,128]{2,1,0:T(8,128)(2,1)S(1)}, bf16[48,128,128]{2,1,0:T(8,128)(2,1)S(1)}, bf16[32,192,128]{2,1,0:T(8,128)(2,1)S(1)}) custom-call(s32[16,48]{1,0:T(8,128)} %bitcast.13, f32[3]{0:T(128)} %coeffs_hbm.1, s32[1,128]{1,0:T(1,128)} %bitcast.14, bf16[48,16,128,128]{3,2,1,0:T(8,128)(2,1)} %h_hbm.1, bf16[48,128,128]{2,1,0:T(8,128)(2,1)} %bitcast.11, ...), custom_call_target="tpu_custom_call" | custom-call | tf_op jit(solution)/shard_map/whole/pallas_call | solution.py:415
  90.7 2.7 %finish.1 = (bf16[48,128,128]{2,1,0:T(8,128)(2,1)}, bf16[48,128,128]{2,1,0:T(8,128)(2,1)}, f32[32,192,128]{2,1,0:T(8,128)}) custom-call(bf16[48,128,128]{2,1,0:T(8,128)(2,1)S(1)} %get-tuple-element.9.next_ref, bf16[48,128,128]{2,1,0:T(8,128)(2,1)S(1)} %get-tuple-element.10.last_ref, bf16[32,192,128]{2,1,0:T(8,128)(2,1)S(1)} %get-tuple-element.11.arrived), custom_call_target="tpu_custom_call" | custom-call | tf_op jit(solution)/shard_map/finish/pallas_call | solution.py:383
